TPU v7x, 256 devices: a whole 4x4x8 slice. The times are simulated.
256 devices in a mesh: rep: 2 (over core), req: 32 (over y, z), tp: 4 (over x).
Axes of the slice: x: 4, y: 4, z: 8, core: 2. Of those that a mesh axis runs over, the one named last changes fastest.
Arguments:
- hidden: bfloat16 [1024, 1536], P(('rep', 'req'), 'tp'), may hold values from -6 to 6
- lengths: int32 [2, 512], P(None, 'req'), may hold values from 16 to 1024, as said below
- migrate: int32 [32], P('req'), may hold values from 0 to 15
- kv_cache: bfloat16 [1024, 1024, 8, 128], P(('rep', 'req'), None, 'tp'), may hold values from -250 to 250
- attn_gain: float32 [1536], replicated, may hold values from 0.1 to 1.9
- moe_gain: float32 [1536], replicated, may hold values from 0.1 to 1.9
- w_query: bfloat16 [1536, 1536], P(None, 'tp'), may hold values from -0.15625 to 0.15625
- key_value_weight: bfloat16 [1536, 1024], P(None, 'tp'), may hold values from -0.15625 to 0.15625
- output_weight: bfloat16 [1536, 1536], P('tp'), may hold values from -0.25 to 0.25
- w_gateup: bfloat16 [64, 1536, 2, 512], P(('rep', 'req'), None, None, 'tp'), may hold values from -0.15625 to 0.15625
- w_down: bfloat16 [64, 512, 1536], P(('rep', 'req'), 'tp'), may hold values from -0.25 to 0.25
- expert_ids: int32 [1024, 8], P(('rep', 'req')), may hold values from 0 to 63, all different within a row; in each aligned block of 16 rows (0 to 15, 16 to 31, ...) at most 6 rows name the same one
- expert_gates: float32 [1024, 8], P(('rep', 'req')), may hold values from 0.1 to 0.4
Outputs:
- layer_out: bfloat16 [1024, 1536], P(('rep', 'req'), 'tp')
Inputs may be any that keep to these rules, and one draw needn't show every extreme that they name: A request attends to its first lengths positions and to its own new key. `expert_ids`: each row names 8 distinct experts; among the rows of one device (an aligned block of 16 rows) no expert is named more than 6 times, and in some blocks one expert is named exactly 6 times.
All inputs are finite; a program needn't handle non-finite values.
Results may differ from a plain program's by a relative error of at most 0.015.
Values may be sent and summed in bfloat16 or wider, within the bound.
A program may use at most 64 MiB of HBM per device.

v0:
```python
import jax
import jax.numpy as jnp
from jax import lax
from jax.sharding import PartitionSpec as P

HEAD_SIZE = 64
epsilon = 1e-06
rope_base = 10000.0
masked_score = -1e30


def swapped(value, axis, apart):
    return lax.ppermute(value, axis, [(i, i ^ 1 << apart) for i in range(lax.axis_size(axis))])


def rms_norm(values, gain):
    mean_square = jnp.mean(values * values, axis=-1, keepdims=True)
    return values * lax.rsqrt(mean_square + epsilon) * gain


def apply_rotation(values, position):
    half_width = values.shape[-1] // 2
    inv_freq = rope_base ** (-jnp.arange(half_width, dtype=jnp.float32) * 2.0 / values.shape[-1])
    angles = position.astype(jnp.float32)[:, None, None] * inv_freq
    cosine = jnp.cos(angles)
    sine_part = jnp.sin(angles)
    first_half = values[..., :half_width]
    second_half = values[..., half_width:]
    return jnp.concatenate(
        [
            first_half * cosine - second_half * sine_part,
            second_half * cosine + first_half * sine_part,
        ],
        axis=-1,
    )


def attention(
    token_part, kv_rows, request_extent, attn_gain, w_query, key_value_weight, output_weight
):
    tokens = lax.all_gather(token_part, "tp", axis=1, tiled=True)
    row_count = tokens.shape[0]
    head_dim = HEAD_SIZE
    local_kv = kv_rows.shape[2]
    local_query = w_query.shape[1] // head_dim
    group_size = local_query // local_kv
    normalized_input = rms_norm(tokens.astype(jnp.float32), attn_gain).astype(jnp.bfloat16)
    query_vectors = jnp.dot(normalized_input, w_query, preferred_element_type=jnp.float32).reshape(
        row_count, local_query, head_dim
    )
    key_value_rows = jnp.dot(
        normalized_input, key_value_weight, preferred_element_type=jnp.float32
    ).reshape(row_count, local_kv, 2 * head_dim)
    query_vectors = (
        apply_rotation(query_vectors, request_extent)
        .astype(jnp.bfloat16)
        .reshape(row_count, local_kv, group_size, head_dim)
    )
    key_new = apply_rotation(key_value_rows[..., :head_dim], request_extent).astype(jnp.bfloat16)
    value_new = key_value_rows[..., head_dim:].astype(jnp.bfloat16)
    score_scale = head_dim ** (-0.5)
    cache_keys = kv_rows[..., :head_dim]
    cache_values = kv_rows[..., head_dim:]
    scores = (
        jnp.einsum("rhgd,rthd->rhgt", query_vectors, cache_keys, preferred_element_type=jnp.float32)
        * score_scale
    )
    own_score = (
        jnp.einsum("rhgd,rhd->rhg", query_vectors, key_new, preferred_element_type=jnp.float32)
        * score_scale
    )
    positions = jnp.arange(kv_rows.shape[1], dtype=jnp.int32)
    visible = positions[None, None, None, :] < request_extent[:, None, None, None]
    scores = jnp.where(visible, scores, masked_score)
    row_peak = jnp.maximum(jnp.max(scores, axis=-1), own_score)
    cache_prob = jnp.exp(scores - row_peak[..., None])
    own_prob = jnp.exp(own_score - row_peak)
    denominator = jnp.sum(cache_prob, axis=-1) + own_prob
    cache_weight = (cache_prob / denominator[..., None]).astype(jnp.bfloat16)
    own_weight = (own_prob / denominator).astype(jnp.bfloat16)
    mixture = jnp.einsum(
        "rhgt,rthd->rhgd", cache_weight, cache_values, preferred_element_type=jnp.float32
    )
    mixture = (
        mixture
        + own_weight.astype(jnp.float32)[..., None] * value_new.astype(jnp.float32)[:, :, None, :]
    )
    context = mixture.reshape(row_count, local_query * head_dim).astype(jnp.bfloat16)
    partial_out = jnp.dot(context, output_weight, preferred_element_type=jnp.float32)
    return tokens.astype(jnp.float32) + lax.psum(partial_out.astype(jnp.bfloat16), "tp").astype(
        jnp.float32
    )


def shards(
    hidden,
    lengths,
    migrate,
    kv_cache,
    attn_gain,
    moe_gain,
    w_query,
    key_value_weight,
    output_weight,
    w_gateup,
    w_down,
    expert_ids,
    expert_gates,
):
    row_count = hidden.shape[0]
    replica = lax.axis_index("rep")
    slot_index = jnp.arange(row_count, dtype=jnp.int32)
    chosen_slot = migrate[0]
    is_moved = slot_index == chosen_slot
    own_span = lax.dynamic_index_in_dim(lengths, replica, 0, keepdims=False)
    other_span = lax.dynamic_index_in_dim(lengths, 1 - replica, 0, keepdims=False)
    picked_cache = lax.dynamic_slice_in_dim(kv_cache, chosen_slot, 1, 0)
    picked_row = lax.dynamic_slice_in_dim(hidden, chosen_slot, 1, 0)
    cache_width = picked_cache.size
    packed = jnp.concatenate([picked_cache.reshape(1, cache_width), picked_row], axis=1)
    arrived = swapped(packed, "rep", 0)
    moved_cache = arrived[:, :cache_width].reshape(picked_cache.shape)
    moved_row = arrived[:, cache_width:]
    served_cache = lax.dynamic_update_slice_in_dim(kv_cache, moved_cache, chosen_slot, 0)
    served_rows = lax.dynamic_update_slice_in_dim(hidden, moved_row, chosen_slot, 0)
    request_extent = jnp.where(is_moved, other_span, own_span)
    residual = attention(
        served_rows,
        served_cache,
        request_extent,
        attn_gain,
        w_query,
        key_value_weight,
        output_weight,
    )
    full_width = moe_gain.shape[0]
    quarter = full_width // lax.axis_size("tp")
    expert_in = rms_norm(residual, moe_gain).astype(jnp.bfloat16)
    own_residual = lax.dynamic_slice_in_dim(residual, lax.axis_index("tp") * quarter, quarter, 1)
    expert_count = lax.axis_size("rep") * lax.axis_size("req")
    top_count = expert_ids.shape[1]
    capacity = min(row_count, max(3, 3 * row_count * top_count // expert_count))
    flat_ids = expert_ids.reshape(-1)
    matches = (flat_ids[:, None] == jnp.arange(expert_count, dtype=jnp.int32)[None, :]).astype(
        jnp.int32
    )
    slot_rank = jnp.sum((jnp.cumsum(matches, axis=0) - matches) * matches, axis=1)
    slot_target = flat_ids * capacity + slot_rank
    slot_table = (
        slot_target[:, None] == jnp.arange(expert_count * capacity, dtype=jnp.int32)[None, :]
    ).astype(jnp.float32)
    route_table = slot_table.reshape(row_count, top_count, -1).sum(axis=1)
    gate_table = (
        (slot_table * expert_gates.reshape(-1, 1)).reshape(row_count, top_count, -1).sum(axis=1)
    )
    outbound = jnp.einsum(
        "rs,rd->sd", route_table.astype(jnp.bfloat16), expert_in, preferred_element_type=jnp.float32
    ).astype(jnp.bfloat16)
    outbound = outbound.reshape(expert_count, capacity, -1)
    gate_up = w_gateup[0].reshape(w_gateup.shape[1], -1)
    down_rows = w_down[0]
    arrived_rows = lax.all_to_all(outbound, ("rep", "req"), split_axis=0, concat_axis=0, tiled=True)
    model_width = arrived_rows.shape[2]
    flattened = arrived_rows.reshape(-1, model_width)
    projected = jnp.dot(flattened, gate_up, preferred_element_type=jnp.float32)
    split_at = projected.shape[1] // 2
    activation = (jax.nn.silu(projected[:, :split_at]) * projected[:, split_at:]).astype(
        jnp.bfloat16
    )
    expert_part = jnp.dot(activation, down_rows, preferred_element_type=jnp.float32)
    expert_part = expert_part.reshape(arrived_rows.shape[0], arrived_rows.shape[1], model_width)
    returned = lax.all_to_all(
        expert_part.astype(jnp.bfloat16), ("rep", "req"), split_axis=0, concat_axis=0, tiled=True
    ).astype(expert_part.dtype)
    returned_rows = returned.reshape(expert_count * capacity, -1)
    combined = jnp.dot(
        gate_table,
        returned_rows,
        precision=lax.Precision.HIGHEST,
        preferred_element_type=jnp.float32,
    )
    expert_mix = lax.psum_scatter(
        combined.astype(jnp.bfloat16), "tp", scatter_dimension=1, tiled=True
    ).astype(jnp.float32)
    return (own_residual + expert_mix).astype(jnp.bfloat16)


def solution(mesh):
    placed = (
        P(("rep", "req"), "tp"),
        P(None, "req"),
        P("req"),
        P(("rep", "req"), None, "tp", None),
        P(),
        P(),
        P(None, "tp"),
        P(None, "tp"),
        P("tp", None),
        P(("rep", "req"), None, None, "tp"),
        P(("rep", "req"), "tp", None),
        P(("rep", "req"), None),
        P(("rep", "req"), None),
    )
    return jax.shard_map(
        shards, mesh=mesh, in_specs=placed, out_specs=P(("rep", "req"), "tp"), check_vma=False
    )
```

profile of v0, /device:TPU:8, one launch (start us, length us, event | category | flops | bytes accessed | tf_op | source)
XLA Modules:
  0.0 226.3 jit_solution(14845780851035790938)
XLA Ops:
  6.5 0.8 copy.69
  8.0 1.4 constant_dynamic-slice_fusion.3
  9.6 4.4 %pad_maximum_fusion = bf16[1,262528]{1,0:T(2,128)(2,1)S(1)} fusion(bf16[1,384]{1,0:T(2,128)(2,1)S(1)} %constant_dynamic-slice_fusion.2, bf16[1,262144]{1,0:T(2,128)(2,1)S(1)} %reshape.200), kind=kLoop, calls=%fused_computation.12 | loop fusion | flops 1050112 | bytes 1050112 | tf_op jit(solution)/shard_map/concatenate | solution.py:120
  14.2 21.2 %copy.45 = bf16[16,1024,2,128]{1,3,2,0:T(8,128)(2,1)} copy(bf16[16,1024,2,128]{3,2,1,0:T(2,128)(2,1)} %param.16) | data formatting | bytes 16777216 | tf_op args[3]
  36.1 0.2 convert_reduce_fusion
  36.6 1.0 copy-done.2
  37.7 12.2 %all_gather.3 = bf16[16,1536]{1,0:T(8,128)(2,1)S(1)} all-gather(bf16[16,384]{1,0:T(8,128)(2,1)S(1)} %dynamic_update_slice.6), channel_id=1, replica_groups=mesh['rep'=2,'req'=32,'tp'=4] {'tp'}, dimensions={1}, use_global_device_ids=true | all-gather | bytes 61440 | tf_op jit(solution)/shard_map/all_gather | solution.py:41
  49.9 9.9 %slice_reduce_fusion = bf16[262144]{0:T(1024)(128)(2,1)S(1)} fusion(bf16[1,262528]{1,0:T(2,128)(2,1)} %copy-done.2), kind=kLoop, calls=%fused_computation.13 | loop fusion | bytes 1048576 | tf_op jit(solution)/shard_map/slice | solution.py:122
  59.8 0.4 copy.46
  60.4 0.3 fusion.36
  60.8 1.4 fusion.34
  62.5 0.9 constant_dynamic-update-slice_fusion
  63.5 0.2 fusion.31
  63.7 3.0 %fusion.44 = (f32[16,2,3]{2,1,0:T(2,128)S(1)}, f32[16,2,3,1024]{3,2,1,0:T(4,128)S(1)}) fusion(bf16[16,1024,2,128]{1,3,2,0:T(8,128)(2,1)} %constant_dynamic-update-slice_fusion, bf16[16,2,3,32]{3,2,1,0:T(4,128)(2,1)S(1)} %copy.44, bf16[16,2,3,32]{3,2,1,0:T(4,128)(2,1)S(1)} %copy.43, pred[16,1024]{1,0:T(8,128)(4,1)S(1)} %iota_compare_fusion.2), kind=kOutput, calls=%fused_computation.77 | convolution fusion | flops 12902304 | bytes 4616576 | tf_op jit(solution)/shard_map/rhgd,rthd->rhgt/dot_general | solution.py:65
  66.8 0.3 fusion.19
  67.2 3.5 %fusion.13 = bf16[16,2,3,64]{3,2,1,0:T(4,128)(2,1)S(1)} fusion(bf16[16,1024,2,128]{1,3,2,0:T(8,128)(2,1)} %constant_dynamic-update-slice_fusion, f32[16,2,3,1024]{3,2,1,0:T(4,128)S(1)} %get-tuple-element.20, f32[16,2,3]{2,1,0:T(2,128)S(1)} %get-tuple-element.14, f32[16,2,3]{2,1,0:T(2,128)S(1)} %multiply_maximum_fusion, f32[16,2,64]{2,1,0:T(2,128)S(1)} %fusion.38, ...), kind=kOutput, calls=%fused_computation.11 | convolution fusion | flops 12896256 | bytes 4609152 | tf_op jit(solution)/shard_map/rhgt,rthd->rhgd/dot_general | solution.py:81
  70.7 0.3 convolution_convert_fusion.3
  71.0 17.0 %psum.7 = bf16[16,1536]{1,0:T(8,128)(2,1)S(1)} all-reduce(bf16[16,1536]{1,0:T(8,128)(2,1)S(1)} %convolution_convert_fusion.3), channel_id=1, replica_groups=mesh['rep'=2,'req'=32,'tp'=4] {'tp'}, use_global_device_ids=true, to_apply=%region_3.4 | all-reduce | flops 24576 | bytes 98304 | tf_op jit(solution)/shard_map/psum | solution.py:90
  88.2 1.5 convolution_convert_fusion
  89.7 2.2 reshape.204
  91.9 51.9 %all_to_all.10 = bf16[64,6,1536]{2,1,0:T(8,128)(2,1)} all-to-all(bf16[64,6,1536]{2,1,0:T(8,128)(2,1)S(1)} %reshape.204), channel_id=1, replica_groups=mesh['rep'=2,'req'=32,'tp'=4] {'rep','req'}, dimensions={0} | all-to-all | bytes 2359296 | tf_op jit(solution)/shard_map/all_to_all | solution.py:162
  143.8 2.3 %reshape.205 = bf16[384,1536]{1,0:T(8,128)(2,1)S(1)} reshape(bf16[64,6,1536]{2,1,0:T(8,128)(2,1)} %all_to_all.10) | data formatting | bytes 2359296 | tf_op jit(solution)/shard_map/reshape | solution.py:164
  146.1 1.7 fusion.16
  147.9 0.4 convolution_convert_fusion.1
  148.4 0.7 copy.51
  149.0 45.9 %all_to_all.11 = bf16[64,6,1536]{2,1,0:T(8,128)(2,1)S(1)} all-to-all(bf16[64,6,1536]{2,1,0:T(8,128)(2,1)S(1)} %copy.51), channel_id=1, replica_groups=mesh['rep'=2,'req'=32,'tp'=4] {'rep','req'}, dimensions={0} | all-to-all | bytes 2359296 | tf_op jit(solution)/shard_map/all_to_all | solution.py:172
  195.0 1.2 reshape.206
  196.2 1.8 convolution_convert_fusion.2
  198.0 0.9 copy.54
  199.0 18.9 %reduce-scatter.4.cloned.1.call-done = bf16[384,16]{1,0:T(8,128)(2,1)} async-done(((bf16[1536,16]{1,0:T(8,128)(2,1)}), bf16[384,16]{1,0:T(8,128)(2,1)}) %reduce-scatter.4.cloned.1.call-update) | async-done | bytes 12304
  217.9 1.0 copy.55
  218.9 0.6 add_convert_fusion.1
  (56 shorter events, 2.4 us)
Async XLA Ops:
  6.5 64.2 %copy-start = (bf16[384,1536]{1,0:T(8,128)(2,1)S(1)}, bf16[384,1536]{1,0:T(8,128)(2,1)}, u32[]{:S(2)}) copy-start(bf16[384,1536]{1,0:T(8,128)(2,1)} %param.21) | copy-start | bytes 3538948
  6.5 211.4 %reduce-scatter.4.cloned.1.call-start = ((), (), s32[]{:S(2)}) async-start(), calls=%async_computation.3 | async-start | bytes 491520
  14.0 21.3 %copy-start.6 = (s32[16,8]{0,1:T(8,128)S(1)}, s32[16,8]{0,1:T(8,128)}, u32[]{:S(2)}) copy-start(s32[16,8]{0,1:T(8,128)} %param.24) | copy-start | bytes 1540
  14.1 22.0 %copy-start.7 = (f32[16,8]{0,1:T(8,128)S(1)}, f32[16,8]{0,1:T(8,128)}, u32[]{:S(2)}) copy-start(f32[16,8]{0,1:T(8,128)} %param.25) | copy-start | bytes 1540
  14.1 22.3 %copy-start.8 = (s32[2,16]{1,0:T(2,128)S(1)}, s32[2,16]{1,0:T(2,128)}, u32[]{:S(2)}) copy-start(s32[2,16]{1,0:T(2,128)} %param.14) | copy-start | bytes 388
  14.1 22.5 %collective-permute-start = (bf16[1,262528]{1,0:T(2,128)(2,1)S(1)}, bf16[1,262528]{1,0:T(2,128)(2,1)S(1)}, u32[]{:S(2)}, u32[]{:S(2)}) collective-permute-start(bf16[1,262528]{1,0:T(2,128)(2,1)S(1)} %pad_maximum_fusion), channel_id=1, source_target_pairs={{0,128},{128,0},{1,129},{129,1},{2,130},{130,2},{3,131},{131,3},{4... | collective-permute-start | bytes 1575176 | tf_op jit(solution)/shard_map/ppermute | solution.py:13
  36.6 1.1 copy-start.2
  49.9 10.4 %copy-start.1 = (bf16[1536,384]{1,0:T(8,128)(2,1)S(1)}, bf16[1536,384]{1,0:T(8,128)(2,1)}, u32[]{:S(2)}) copy-start(bf16[1536,384]{1,0:T(8,128)(2,1)} %param.19) | copy-start | bytes 3538948
  49.9 10.4 %copy-start.4 = (f32[1536]{0:T(1024)S(1)}, f32[1536]{0:T(1024)}, u32[]{:S(2)}) copy-start(f32[1536]{0:T(1024)} %param.17) | copy-start | bytes 18436
  70.6 17.6 %copy-start.5 = (f32[1536]{0:T(1024)S(1)}, f32[1536]{0:T(1024)}, u32[]{:S(2)}) copy-start(f32[1536]{0:T(1024)} %param.18) | copy-start | bytes 18436
  146.1 1.8 copy-start.3
Sparse Core Ops, SparseCore 0:
  199.1 18.7 reduce-scatter.3
where the time goes:
time: 227 us; the launch traced here: 226 us
  blocking collectives  127 us (56%)
  local copies, waits for them, and re-layouts  44.7 us (20%)
  waiting for transfers between devices  18.9 us (8%)
  between operations  14.4 us (6%)
  matrix products  14.1 us (6%)
  other arithmetic  6.97 us (3%)
    all_to_all x1, blocking collectives, shards(): lax.all_to_all(outbound, ('rep', 'req'), split_axis=0, concat_axis=0, til...  51.9 us
    all_to_all x1, blocking collectives, shards(): lax.all_to_all(expert_part.astype(jnp.bfloat16), ('rep', 'req'), split_ax...  45.9 us
    unnamed x24, local copies, waits for them, and re-layouts  25.1 us
    unnamed x2, waiting for transfers between devices  18.9 us
    psum x1, blocking collectives, attention(): lax.psum(partial_out.astype(jnp.bfloat16), 'tp').astype(jnp.float32)  17 us
    all_gather x1, blocking collectives, attention(): tokens = lax.all_gather(token_part, 'tp', axis=1, tiled=True)  12.2 us
    slice x1, local copies, waits for them, and re-layouts, shards(): moved_cache = arrived[:, :cache_width].reshape(picked_cache.shape)  9.86 us
  transfers between devices with their start and end apart: 2, of which 1 were waited for; matrix products, arithmetic and copies ran while one was open for 10% of the time, Pallas kernels for 0%

commit v1 on v0

--- a/solution.py
+++ b/solution.py
@@ -38,7 +38,10 @@
 def attention(
     token_part, kv_rows, request_extent, attn_gain, w_query, key_value_weight, output_weight
 ):
-    tokens = lax.all_gather(token_part, "tp", axis=1, tiled=True)
+    devices = lax.axis_size("tp")
+    blocks = jnp.stack([token_part for _ in range(devices)])
+    blocks = lax.all_to_all(blocks, "tp", split_axis=0, concat_axis=0)
+    tokens = jnp.concatenate(blocks, axis=1)
     row_count = tokens.shape[0]
     head_dim = HEAD_SIZE
     local_kv = kv_rows.shape[2]

time: 227 us -> 224 us (0.987)
  blocking collectives: 127 us -> 116 us
  local copies, waits for them, and re-layouts: 44.7 us -> 50.2 us
  starting transfers between devices: 0.09 us -> 4.3 us
  matrix products: 14.1 us -> 11.7 us
    all_gather x1 -> x0, blocking collectives: 12.2 us -> none  [attention(): tokens = lax.all_gather(token_part, 'tp', axis=1, tiled=True)]
    all_to_all x0 -> x1, starting transfers between devices: none -> 4.29 us  [attention(): blocks = lax.all_to_all(blocks, 'tp', split_axis=0, concat_axis=0)]
    unnamed x24 -> x25, local copies, waits for them, and re-layouts: 25.1 us -> 25.7 us
  transfers between devices with their start and end apart: 2 -> 3, of which waited for: 1 -> 1; matrix products, arithmetic and copies ran while one was open for 10% -> 17% of each run, Pallas kernels for 0% -> 0%
where the time goes in v1:
time: 224 us; the launch traced here: 223 us
  blocking collectives  116 us (52%)
  local copies, waits for them, and re-layouts  50.2 us (22%)
  waiting for transfers between devices  19 us (8%)
  between operations  14.4 us (6%)
  matrix products  11.7 us (5%)
  other arithmetic  7.8 us (3%)
  starting transfers between devices  4.3 us (2%)
    all_to_all x1, blocking collectives, shards(): lax.all_to_all(outbound, ('rep', 'req'), split_axis=0, concat_axis=0, til...  51.9 us
    all_to_all x1, blocking collectives, shards(): lax.all_to_all(expert_part.astype(jnp.bfloat16), ('rep', 'req'), split_ax...  45.9 us
    unnamed x25, local copies, waits for them, and re-layouts  25.7 us
    unnamed x2, waiting for transfers between devices  19 us
    psum x1, blocking collectives, attention(): lax.psum(partial_out.astype(jnp.bfloat16), 'tp').astype(jnp.float32)  17.9 us
    slice x1, local copies, waits for them, and re-layouts, shards(): moved_cache = arrived[:, :cache_width].reshape(picked_cache.shape)  10.6 us
    concatenate x1, other arithmetic, shards(): jnp.concatenate([picked_cache.reshape(1, cache_width), picked_row], axis=1)  5.14 us
  transfers between devices with their start and end apart: 3, of which 1 were waited for; matrix products, arithmetic and copies ran while one was open for 17% of the time, Pallas kernels for 0%

profile of v1, /device:TPU:8, one launch (start us, length us, event | category | flops | bytes accessed | tf_op | source)
XLA Modules:
  0.0 223.1 jit_solution(6973093702660996492)
XLA Ops:
  6.5 0.8 copy.96
  8.0 1.4 constant_dynamic-slice_fusion.3
  9.6 5.1 %pad_maximum_fusion = bf16[1,262528]{1,0:T(2,128)(2,1)} fusion(bf16[1,384]{1,0:T(2,128)(2,1)S(1)} %constant_dynamic-slice_fusion.2, bf16[1,262144]{1,0:T(2,128)(2,1)S(1)} %reshape.230), kind=kLoop, calls=%fused_computation.12 | loop fusion | flops 1050112 | bytes 1050112 | tf_op jit(solution)/shard_map/concatenate | solution.py:123
  14.8 21.2 %copy.68 = bf16[16,1024,2,128]{1,3,2,0:T(8,128)(2,1)} copy(bf16[16,1024,2,128]{3,2,1,0:T(2,128)(2,1)} %param.16) | data formatting | bytes 16777216 | tf_op args[3]
  36.0 0.3 copy.79
  36.3 1.6 copy.65
  39.2 0.7 slice.48
  39.9 0.6 stack.2
  40.5 4.3 %all-to-all-start = ((bf16[4,16,384]{2,1,0:T(8,128)(2,1)}), bf16[4,16,384]{2,1,0:T(8,128)(2,1)S(1)}, u32[]{:S(2)}, u32[]{:S(2)}) async-start(bf16[4,16,384]{2,1,0:T(8,128)(2,1)} %stack.2), calls=%async_computation | async-start | bytes 98304 | tf_op jit(solution)/shard_map/all_to_all | solution.py:43
  44.8 10.6 %slice_reduce_fusion = bf16[262144]{0:T(1024)(128)(2,1)} fusion(bf16[1,262528]{1,0:T(2,128)(2,1)} %collective-permute-done), kind=kLoop, calls=%fused_computation.13 | loop fusion | bytes 1048576 | tf_op jit(solution)/shard_map/slice | solution.py:125
  55.4 2.0 copy.69
  57.4 1.9 constant_dynamic-update-slice_fusion
  59.6 0.3 fusion.43
  59.9 0.6 fusion.42
  61.1 3.7 %fusion.41 = (f32[16,2,3]{2,1,0:T(2,128)S(1)}, f32[16,2,3,1024]{3,2,1,0:T(4,128)S(1)}) fusion(bf16[16,1024,2,128]{1,3,2,0:T(8,128)(2,1)} %constant_dynamic-update-slice_fusion, bf16[16,2,3,32]{3,2,1,0:T(4,128)(2,1)S(1)} %copy.67, bf16[16,2,3,32]{3,2,1,0:T(4,128)(2,1)S(1)} %copy.66, pred[16,1024]{1,0:T(8,128)(4,1)S(1)} %iota_compare_fusion.2), kind=kOutput, calls=%fused_computation.77 | convolution fusion | flops 12902304 | bytes 4616576 | tf_op jit(solution)/shard_map/rhgd,rthd->rhgt/dot_general | solution.py:68
  64.8 0.3 fusion.19
  65.2 1.3 fusion.13
  66.9 17.9 %psum.7 = bf16[16,1536]{1,0:T(8,128)(2,1)S(1)} all-reduce(bf16[16,1536]{1,0:T(8,128)(2,1)S(1)} %convolution_convert_fusion.3), channel_id=1, replica_groups=mesh['rep'=2,'req'=32,'tp'=4] {'tp'}, use_global_device_ids=true, to_apply=%region_3.4 | all-reduce | flops 24576 | bytes 98304 | tf_op jit(solution)/shard_map/psum | solution.py:93
  84.9 1.5 convolution_convert_fusion
  86.4 2.2 reshape.232
  88.6 51.9 %all_to_all.15 = bf16[64,6,1536]{2,1,0:T(8,128)(2,1)} all-to-all(bf16[64,6,1536]{2,1,0:T(8,128)(2,1)S(1)} %reshape.232), channel_id=1, replica_groups=mesh['rep'=2,'req'=32,'tp'=4] {'rep','req'}, dimensions={0} | all-to-all | bytes 2359296 | tf_op jit(solution)/shard_map/all_to_all | solution.py:165
  140.5 2.3 %reshape.233 = bf16[384,1536]{1,0:T(8,128)(2,1)S(1)} reshape(bf16[64,6,1536]{2,1,0:T(8,128)(2,1)} %all_to_all.15) | data formatting | bytes 2359296 | tf_op jit(solution)/shard_map/reshape | solution.py:167
  142.8 1.7 fusion.16
  144.6 0.4 convolution_convert_fusion.1
  145.1 0.7 copy.76
  145.7 45.9 %all_to_all.16 = bf16[64,6,1536]{2,1,0:T(8,128)(2,1)S(1)} all-to-all(bf16[64,6,1536]{2,1,0:T(8,128)(2,1)S(1)} %copy.76), channel_id=1, replica_groups=mesh['rep'=2,'req'=32,'tp'=4] {'rep','req'}, dimensions={0} | all-to-all | bytes 2359296 | tf_op jit(solution)/shard_map/all_to_all | solution.py:175
  191.7 1.2 reshape.234
  192.9 1.8 convolution_convert_fusion.2
  194.7 0.9 copy.80
  195.7 18.9 %reduce-scatter.4.cloned.1.call-done = bf16[384,16]{1,0:T(8,128)(2,1)} async-done(((bf16[1536,16]{1,0:T(8,128)(2,1)}), bf16[384,16]{1,0:T(8,128)(2,1)}) %reduce-scatter.4.cloned.1.call-update) | async-done | bytes 12304
  214.6 1.0 copy.81
  215.6 0.6 add_convert_fusion.1
  (63 shorter events, 3.0 us)
Async XLA Ops:
  6.5 60.1 %copy-start = (bf16[384,1536]{1,0:T(8,128)(2,1)S(1)}, bf16[384,1536]{1,0:T(8,128)(2,1)}, u32[]{:S(2)}) copy-start(bf16[384,1536]{1,0:T(8,128)(2,1)} %param.21) | copy-start | bytes 3538948
  14.8 24.4 %collective-permute-start = (bf16[1,262528]{1,0:T(2,128)(2,1)}, bf16[1,262528]{1,0:T(2,128)(2,1)}, u32[]{:S(2)}, u32[]{:S(2)}) collective-permute-start(bf16[1,262528]{1,0:T(2,128)(2,1)} %pad_maximum_fusion), channel_id=1, source_target_pairs={{0,128},{128,0},{1,129},{129,1},{2,130},{130,2},{3,131},{131,3},{4... | collective-permute-start | bytes 1575176 | tf_op jit(solution)/shard_map/ppermute | solution.py:13
  14.8 21.2 %copy-start.5 = (f32[1536]{0:T(1024)S(1)}, f32[1536]{0:T(1024)}, u32[]{:S(2)}) copy-start(f32[1536]{0:T(1024)} %param.17) | copy-start | bytes 18436
  14.8 21.2 %copy-start.2 = (bf16[1536,256]{1,0:T(8,128)(2,1)S(1)}, bf16[1536,256]{1,0:T(8,128)(2,1)}, u32[]{:S(2)}) copy-start(bf16[1536,256]{1,0:T(8,128)(2,1)} %param.20) | copy-start | bytes 2359300
  36.3 1.6 copy-start.6
  36.3 2.3 %copy-start.7 = (f32[16,8]{0,1:T(8,128)S(1)}, f32[16,8]{0,1:T(8,128)}, u32[]{:S(2)}) copy-start(f32[16,8]{0,1:T(8,128)} %param.25) | copy-start | bytes 1540
  36.3 2.6 %copy-start.8 = (s32[2,16]{1,0:T(2,128)S(1)}, s32[2,16]{1,0:T(2,128)}, u32[]{:S(2)}) copy-start(s32[2,16]{1,0:T(2,128)} %param.14) | copy-start | bytes 388
  40.5 18.8 %all-to-all-start = ((bf16[4,16,384]{2,1,0:T(8,128)(2,1)}), bf16[4,16,384]{2,1,0:T(8,128)(2,1)S(1)}, u32[]{:S(2)}, u32[]{:S(2)}) async-start(bf16[4,16,384]{2,1,0:T(8,128)(2,1)} %stack.2), calls=%async_computation | async-start | bytes 98304 | tf_op jit(solution)/shard_map/all_to_all | solution.py:43
  44.8 169.8 %reduce-scatter.4.cloned.1.call-start = ((), (), s32[]{:S(2)}) async-start(), calls=%async_computation.4 | async-start | bytes 491520
  59.6 5.6 %copy-start.1 = (bf16[16,1024,2,128]{1,3,2,0:T(8,128)(2,1)S(1)}, bf16[16,1024,2,128]{1,3,2,0:T(8,128)(2,1)}, u32[]{:S(2)}) copy-start(bf16[16,1024,2,128]{1,3,2,0:T(8,128)(2,1)} %constant_dynamic-update-slice_fusion) | copy-start | bytes 25165828
  66.5 18.4 %copy-start.4 = (f32[1536]{0:T(1024)S(1)}, f32[1536]{0:T(1024)}, u32[]{:S(2)}) copy-start(f32[1536]{0:T(1024)} %param.18) | copy-start | bytes 18436
  142.8 1.8 copy-start.3
Sparse Core Ops, SparseCore 0:
  195.8 18.7 reduce-scatter.3
